TPU v7x, 512 devices: a whole 4x8x8 slice. The times are simulated.
512 devices in a mesh: dp: 8 (over x, core), vocab: 64 (over y, z).
Axes of the slice: x: 4, y: 8, z: 8, core: 2. Of those that a mesh axis runs over, the one named last changes fastest.
Arguments:
- hidden: bfloat16 [640, 4608], P('dp'), may hold values from -30 to 30
- head_weight: bfloat16 [4608, 262144], P(None, ('dp', 'vocab')), may hold values from -0.09375 to 0.09375
- drafts: int32 [128, 4], replicated, may hold values from 0 to 262143
- cutoffs: int32 [128, 4], P('dp'), may hold values from -30720 to -18433
Outputs:
- log_norm: float32 [128, 5], P('dp')
- draft_logprob: float32 [128, 4], P('dp')
- expected_accept: float32 [128], P('dp')
- z_loss: float32 [], replicated
All inputs are finite; a program needn't handle non-finite values.
Results may differ from a plain program's by a relative error of at most 0.0003.
Values may be sent and summed in bfloat16 or wider, within the bound.
A program may use at most 64 MiB of HBM per device.

v0:
```python
import functools

import jax
import jax.numpy as jnp
from jax import lax
from jax.sharding import Mesh
from jax.sharding import PartitionSpec as P

DRAFTS = 4
POSITIONS = 5
VOCAB = ("vocab_0", "vocab_1")
DP = ("dp_0", "dp_1")
DP_VOCAB = ("dp_0", "dp_1", "vocab_0", "vocab_1")


SOFT_CAP = 30.0
Z_WEIGHT = 0.001


def over_axes(value, axes):
    return functools.reduce(lax.psum, axes, value)


def local(hidden, head_weight, drafts, cutoffs):
    vocab_devices = lax.axis_size(VOCAB)
    shard_index = lax.axis_index(DP) * vocab_devices + lax.axis_index(VOCAB)
    shard_width = head_weight.shape[1]
    offset = shard_index * shard_width
    sentinel = jnp.full((drafts.shape[0], 1), -1, jnp.int32)
    draft_rows = jnp.concatenate([drafts, sentinel], axis=1).reshape(-1)
    local_ids = jnp.where(draft_rows >= 0, draft_rows - offset, -1)
    columns = lax.broadcasted_iota(jnp.int32, (1, shard_width), 1)
    logits = jnp.dot(
        lax.all_gather(hidden, DP, axis=0, tiled=True),
        head_weight,
        preferred_element_type=jnp.float32,
    )
    capped = SOFT_CAP * jnp.tanh(logits / SOFT_CAP)
    exp_total = jnp.sum(jnp.exp(capped), axis=1)
    picked = jnp.sum(jnp.where(columns == local_ids[:, None], capped, 0.0), axis=1)
    partial_value = jnp.stack([exp_total, picked], 0)
    exp_total = partial_value[0]
    picked = partial_value[1]
    own_rows = hidden.shape[0]
    exp_total, picked = (over_axes(exp_total, DP_VOCAB), over_axes(picked, DP_VOCAB))
    log_total = jnp.log(exp_total)
    z_loss = Z_WEIGHT * jnp.mean(log_total * log_total)
    first_own = lax.axis_index(DP) * own_rows
    log_total = lax.dynamic_slice_in_dim(log_total, first_own, own_rows, 0)
    picked = lax.dynamic_slice_in_dim(picked, first_own, own_rows, 0)
    log_norm = log_total.reshape(-1, POSITIONS)
    picks = picked.reshape(-1, POSITIONS)
    draft_logprob = picks[:, :DRAFTS] - log_norm[:, :DRAFTS]
    accept = jax.nn.sigmoid(draft_logprob - cutoffs.astype(jnp.float32) / 1024.0)
    expected_accept = jnp.sum(jnp.cumprod(accept, axis=1), axis=1)
    return (log_norm, draft_logprob, expected_accept, z_loss)


def solution(mesh):
    split = Mesh(mesh.devices.reshape(4, 2, 8, 8), ("dp_0", "dp_1", "vocab_0", "vocab_1"))
    placed = (P(DP, None), P(None, DP_VOCAB), P(), P(DP, None))
    return jax.shard_map(
        local,
        mesh=split,
        in_specs=placed,
        out_specs=(P(DP, None), P(DP, None), P(DP), P()),
        check_vma=False,
    )
```

profile of v0, /device:TPU:2, one launch (start us, length us, event | category | flops | bytes accessed | tf_op | source)
XLA Modules:
  0.0 125.7 jit_solution(16251474849010502258)
XLA Ops:
  7.2 0.0 all-gather.2.cloned.1.call-start
  7.2 0.7 all-gather.2.cloned.1.call-update
  7.9 0.7 fusion.2
  8.6 0.1 copy.11
  8.7 0.2 select_n.21
  8.9 0.8 copy.12
  9.7 48.7 %all-gather.2.cloned.1.call-done = bf16[640,4608]{1,0:T(8,128)(2,1)} async-done(((bf16[80,4608]{1,0:T(8,128)(2,1)}), bf16[640,4608]{1,0:T(8,128)(2,1)}) %all-gather.2.cloned.1.call-update) | async-done | bytes 5898256 | tf_op jit(solution)/shard_map/all_gather | solution.py:34
  58.4 8.2 %select_reduce_fusion = (f32[640]{0:T(1024)S(1)}, f32[640]{0:T(1024)S(1)}) fusion(s32[640]{0:T(1024)S(1)} %select_n.21, bf16[640,4608]{1,0:T(8,128)(2,1)} %all-gather.2.cloned.1.call-done, bf16[4608,512]{1,0:T(8,128)(2,1)} %param.5), kind=kOutput, calls=%fused_computation.3 | convolution fusion | flops 3021863936 | bytes 10624512 | tf_op jit(solution)/shard_map/dot_general | solution.py:33
  66.6 9.3 %all-reduce.3 = (f32[640]{0:T(1024)S(1)}, f32[640]{0:T(1024)S(1)}) all-reduce(f32[640]{0:T(1024)S(1)} %get-tuple-element.13, f32[640]{0:T(1024)S(1)} %get-tuple-element.12), channel_id=1, replica_groups=mesh['dp_0'=4,'dp_1'=2,'vocab_0'=8,'vocab_1'=8] {'dp_0'}, use_global_device_ids=true, to_apply=%region_1.2 | all-reduce | flops 1280 | bytes 10240 | tf_op jit(solution)/shard_map/psum | solution.py:21
  75.9 2.5 %all-reduce.4 = (f32[640]{0:T(1024)S(1)}, f32[640]{0:T(1024)S(1)}) all-reduce(f32[640]{0:T(1024)S(1)} %get-tuple-element.18, f32[640]{0:T(1024)S(1)} %get-tuple-element.19), channel_id=1, replica_groups=mesh['dp_0'=4,'dp_1'=2,'vocab_0'=8,'vocab_1'=8] {'dp_1'}, use_global_device_ids=true, to_apply=%region_2.3 | all-reduce | flops 1280 | bytes 10240 | tf_op jit(solution)/shard_map/psum | solution.py:21
  78.4 17.2 %all-reduce.2 = (f32[640]{0:T(1024)S(1)}, f32[640]{0:T(1024)S(1)}) all-reduce(f32[640]{0:T(1024)S(1)} %get-tuple-element.20, f32[640]{0:T(1024)S(1)} %get-tuple-element.21), channel_id=1, replica_groups=mesh['dp_0'=4,'dp_1'=2,'vocab_0'=8,'vocab_1'=8] {'vocab_0'}, use_global_device_ids=true, to_apply=%region_3.4 | all-reduce | flops 1280 | bytes 10240 | tf_op jit(solution)/shard_map/psum | solution.py:21
  95.6 18.4 %all-reduce.1 = (f32[640]{0:T(1024)S(1)}, f32[640]{0:T(1024)S(1)}) all-reduce(f32[640]{0:T(1024)S(1)} %get-tuple-element.16, f32[640]{0:T(1024)S(1)} %get-tuple-element.17), channel_id=1, replica_groups=mesh['dp_0'=4,'dp_1'=2,'vocab_0'=8,'vocab_1'=8] {'vocab_1'}, use_global_device_ids=true, to_apply=%region_4.5 | all-reduce | flops 1280 | bytes 10240 | tf_op jit(solution)/shard_map/psum | solution.py:21
  114.0 0.1 dynamic_slice.7
  114.0 0.1 reshape.32
  114.1 0.6 multiply_reduce_fusion
  114.7 0.1 dynamic_slice.6
  114.8 0.1 reshape.31
  114.9 0.7 copy.13
  115.6 0.7 copy.14
  116.2 0.2 reduce_window.9
  116.4 0.6 reduce_sum.38
  (1 shorter events, 0.0 us)
Async XLA Ops:
  7.2 51.2 %all-gather.2.cloned.1.call-start = ((), (), s32[]{:S(2)}) async-start(), calls=%async_computation | async-start | bytes 6635520 | tf_op jit(solution)/shard_map/all_gather | solution.py:34
Sparse Core Ops, SparseCore 0:
  10.1 48.2 all-gather.1
where the time goes:
time: 126 us
  waiting for transfers between devices  49.4 us (39%)
  blocking collectives  47.4 us (38%)
  between operations  15.9 us (13%)
  matrix products  8.18 us (6%)
  local copies, waits for them, and re-layouts  2.73 us (2%)
  other arithmetic  2.1 us (2%)
    all_gather x1, waiting for transfers between devices, local(): lax.all_gather(hidden, DP, axis=0, tiled=True)  48.7 us
    psum x4, blocking collectives, over_axes(): return functools.reduce(lax.psum, axes, value)  47.4 us
    dot_general x1, matrix products, local(): jnp.dot(lax.all_gather(hidden, DP, axis=0, tiled=True), head_weight, pref...  8.18 us
  transfers between devices with their start and end apart: 1, of which 1 were waited for; matrix products, arithmetic and copies ran while one was open for 1% of the time, Pallas kernels for 0%

commit v1 on v0

v1 whole, which is shorter than its diff:
```python
import functools

import jax
import jax.numpy as jnp
from jax import lax
from jax.experimental import pallas as pl
from jax.experimental.pallas import tpu as pltpu
from jax.sharding import Mesh
from jax.sharding import PartitionSpec as P

DRAFTS = 4
POSITIONS = 5
AXES = ("x", "core", "y", "z")
NX, NY, NZ = 4, 8, 8
MESH = pl.DeviceIdType.MESH

SOFT_CAP = 30.0
Z_WEIGHT = 0.001

ROWS = 80
WIDTH = 512
TILE = 256
TILES = 18
REGION = 3
DIRECT = 4 * REGION
GROUP = 3


def column_to_row(column, rows):
    at = lax.broadcasted_iota(jnp.int32, (rows, 128), 0)
    lane = lax.broadcasted_iota(jnp.int32, (rows, 128), 1)
    return jnp.sum(jnp.where(at == lane, column, 0.0), axis=0, keepdims=True)


def verify_kernel(
    hidden, weight, drafts, out,
    held, own_w, partner_w, acc_own, acc_partner, ids, part, z_in, plane, xy_in, log_part, log_in,
    load_sem, w_sem, w_send, w_recv, color_recv, color_send, direct_recv, direct_send,
    y_recv, z_recv, plane_send, red_send, red_recv, fin_send, fin_recv,
):
    x, core, y, z = (lax.axis_index(a) for a in AXES)
    step = 1 - 2 * core

    def ahead(n):
        return lax.rem(x + n * step + NX, NX)

    def at(dx=0, dy=0, dz=0):
        return (
            ahead(dx) if dx else x,
            core,
            lax.rem(y + dy + NY, NY) if dy else y,
            lax.rem(z + dz + NZ, NZ) if dz else z,
        )

    partner = (x, 1 - core, y, z)
    colour = lax.rem(y + 2 * z, 4)
    mine = REGION * colour

    def remote(src, dst, send, recv, to):
        copy = pltpu.make_async_remote_copy(
            src_ref=src, dst_ref=dst, send_sem=send, recv_sem=recv, device_id=to, device_id_type=MESH
        )
        copy.start()
        return copy

    for t in range(TILES):
        pltpu.make_async_copy(hidden.at[:, pl.ds(t * TILE, TILE)], held.at[t, 0], load_sem).start()
    load_w = pltpu.make_async_copy(weight, own_w, w_sem)
    load_w.start()

    barrier = pltpu.get_barrier_semaphore()
    peers = [at(dz=d) for d in range(1, NZ)]
    peers += [at(dx=a, dy=b) for a in range(NX) for b in range(NY) if a or b]
    peers.append(partner)
    for peer in peers:
        pl.semaphore_signal(barrier, inc=1, device_id=peer, device_id_type=MESH)
    pl.semaphore_wait(barrier, len(peers))

    pltpu.make_async_copy(held.at[:, 0], held.at[:, 0], load_sem).wait()
    sent = []
    front, back = at(dx=1), at(dx=-1)

    slots = {}
    for i, (to, slot, t) in enumerate(
        [(front, 1, 0), (back, 3, 2), (front, 1, 1), (back, 3, 0), (front, 1, 2), (back, 3, 1)]
    ):
        copy = remote(held.at[mine + t, 0], held.at[mine + t, slot], color_send.at[i], color_recv.at[i], to)
        slots[slot, t] = copy
        sent.append(copy)

    def direct(i, to, source, slot, first):
        tiles = pl.ds(first, GROUP)
        copy = remote(held.at[tiles, source], held.at[tiles, slot], direct_send.at[i], direct_recv.at[i], to)
        sent.append(copy)
        return copy

    low, high = DIRECT, DIRECT + GROUP
    direct_in = [direct(0, front, 0, 1, low), direct(1, back, 0, 3, high)]
    w_copy = remote(weight, partner_w, w_send, w_recv, partner)
    sent.append(w_copy)

    row = lax.broadcasted_iota(jnp.int32, (ROWS, 128), 0)
    lane = lax.broadcasted_iota(jnp.int32, (ROWS, 128), 1)
    for slot in range(NX):
        block = 2 * ahead(-slot) + core if slot else 2 * x + core
        chosen = drafts[pl.ds(pl.multiple_of(16 * block, 16), 16), :].astype(jnp.float32)
        spread = jnp.zeros((ROWS, 128), jnp.float32)
        for p in range(DRAFTS):
            here = row == lane * POSITIONS + p
            spread += jnp.where(here, column_to_row(chosen[:, p : p + 1], 16), 0.0)
        found = jnp.sum(spread, axis=1, keepdims=True)
        bonus = lax.rem(lax.broadcasted_iota(jnp.int32, (ROWS, 1), 0), POSITIONS) == DRAFTS
        ids[slot] = jnp.broadcast_to(jnp.where(bonus, -1.0, found), (ROWS, 128))

    plane_count = [0]

    def forward(slot, t):
        piece = held.at[mine + t, slot]
        toward = at(dz=1) if t < 2 else at(dz=-1)
        for to, sem in ((at(dy=1), y_recv.at[0, t]), (at(dy=-1), y_recv.at[1, t]), (toward, z_recv.at[t])):
            sent.append(remote(piece, piece, plane_send.at[plane_count[0]], sem, to))
            plane_count[0] += 1

    relays = {(1, 0): front, (3, 2): back, (1, 1): front}
    for slot, t in [(1, 0), (3, 2), (1, 1), (3, 0), (1, 2), (3, 1)]:
        slots[slot, t].wait_recv()
        if (slot, t) in relays:
            i = 6 + t
            copy = remote(
                held.at[mine + t, slot], held.at[mine + t, 2], color_send.at[i], color_recv.at[i], relays[slot, t]
            )
            slots[2, t] = copy
            sent.append(copy)
        forward(slot, t)
    direct_in += [direct(2, front, 0, 1, high), direct(3, back, 0, 3, low)]
    direct_in[0].wait_recv()
    direct_in.append(direct(4, front, 1, 2, low))
    direct_in[1].wait_recv()
    direct_in.append(direct(5, back, 3, 2, high))
    for t in (0, 2, 1):
        slots[2, t].wait_recv()
        forward(2, t)

    load_w.wait()
    w_copy.wait_recv()

    def multiply(first, start=False):
        for weights, total in ((own_w, acc_own), (partner_w, acc_partner)):
            value = None if start else total[...]
            for t in range(REGION):
                rows = pl.ds(pl.multiple_of((first + t) * TILE, TILE), TILE)
                product = jnp.dot(
                    held[first + t].reshape(NX * ROWS, TILE),
                    weights[rows, :],
                    preferred_element_type=jnp.float32,
                )
                value = product if value is None else value + product
            total[...] = value

    def arrived(first, t, sem):
        piece = held.at[first + t, pl.ds(1, NX - 1)]
        pltpu.make_async_copy(piece, piece, sem).wait()

    multiply(mine, start=True)
    other = REGION * lax.rem(colour + 2, 4)
    for t in range(REGION):
        arrived(other, t, z_recv.at[t])
    multiply(other)
    direct_in[3].wait_recv()
    direct_in[4].wait_recv()
    multiply(low)
    direct_in[2].wait_recv()
    direct_in[5].wait_recv()
    multiply(high)
    for k, shift in ((0, 3), (1, 1)):
        other = REGION * lax.rem(colour + shift, 4)
        for t in range(REGION):
            arrived(other, t, y_recv.at[k, t])
        multiply(other)

    vocab = y * NZ + z
    columns = lax.broadcasted_iota(jnp.int32, (ROWS, 128), 1)
    for slot in range(NX):
        exp_sum = jnp.zeros((ROWS, 128), jnp.float32)
        pick_sum = jnp.zeros((ROWS, 128), jnp.float32)
        wanted = ids[slot].astype(jnp.int32)
        for total, at_core in ((acc_own, core), (acc_partner, 1 - core)):
            offset = ((2 * x + at_core) * (NY * NZ) + vocab) * WIDTH
            for j in range(WIDTH // 128):
                logits = total[pl.ds(slot * ROWS, ROWS), pl.ds(j * 128, 128)]
                capped = SOFT_CAP * jnp.tanh(logits * (1.0 / SOFT_CAP))
                exp_sum += jnp.exp(capped)
                pick_sum += jnp.where(columns + (offset + j * 128) == wanted, capped, 0.0)
        part[pl.ds(slot, 1), :] = column_to_row(jnp.sum(exp_sum, axis=1, keepdims=True), ROWS)
        part[pl.ds(NX + slot, 1), :] = column_to_row(jnp.sum(pick_sum, axis=1, keepdims=True), ROWS)

    for d in range(1, NZ):
        remote(part, z_in.at[d - 1], red_send.at[0], red_recv.at[0], at(dz=d))
    pltpu.make_async_copy(z_in, z_in, red_recv.at[0]).wait()
    plane[...] = part[...] + jnp.sum(z_in[...], axis=0)
    n = NX * NY - 1
    for a in range(NX):
        for b in range(NY):
            if a or b:
                remote(plane, xy_in.at[a * NY + b - 1], red_send.at[1], red_recv.at[1], at(dx=a, dy=b))
    pltpu.make_async_copy(xy_in, xy_in, red_recv.at[1]).wait()
    from_x = []
    for a in range(NX):
        first = max(a * NY - 1, 0)
        count = NY if a else NY - 1
        value = jnp.sum(xy_in[pl.ds(first, count)], axis=0)
        from_x.append(value + plane[...] if a == 0 else value)
    totals = []
    for slot in range(NX):
        value = from_x[0][slot : slot + 1]
        for a in range(1, NX):
            k = (slot - a) % NX
            value += from_x[a][k : k + 1]
        totals.append(value)
    picked = from_x[0][NX : NX + 1]
    for a in range(1, NX):
        k = NX + (-a) % NX
        picked += from_x[a][k : k + 1]
    valid = lax.broadcasted_iota(jnp.int32, (1, 128), 1) < ROWS
    logs = [jnp.log(jnp.where(valid, value, 1.0)) for value in totals]
    squares = functools.reduce(jnp.add, [value * value for value in logs])
    log_part[...] = jnp.broadcast_to(squares, (8, 128))
    fin = remote(log_part, log_in, fin_send, fin_recv, partner)
    out[pl.ds(0, 1), :] = logs[0]
    out[pl.ds(1, 1), :] = picked
    fin.wait_recv()
    out[pl.ds(2, 1), :] = squares + log_in[pl.ds(0, 1), :]
    out[pl.ds(3, 5), :] = jnp.zeros((5, 128), jnp.float32)

    fin.wait_send()
    pltpu.make_async_copy(z_in, z_in, red_send.at[0]).wait()
    pltpu.make_async_copy(xy_in, xy_in, red_send.at[1]).wait()
    for copy in sent:
        copy.wait_send()


def finish_kernel(packed, cutoffs, log_norm, draft_logprob, expected, z_loss):
    seqs = 16
    at = lax.broadcasted_iota(jnp.int32, (seqs, 128), 0)
    lane = lax.broadcasted_iota(jnp.int32, (seqs, 128), 1)
    logs, picked, squares = packed[0:1], packed[1:2], packed[2:3]
    limits = cutoffs[...].astype(jnp.float32) * (1.0 / 1024.0)
    product = jnp.ones((seqs, 1), jnp.float32)
    total = jnp.zeros((seqs, 1), jnp.float32)
    for p in range(POSITIONS):
        here = lane == at * POSITIONS + p
        log_p = jnp.sum(jnp.where(here, logs, 0.0), axis=1, keepdims=True)
        log_norm[:, p : p + 1] = log_p
        if p < DRAFTS:
            draft = jnp.sum(jnp.where(here, picked, 0.0), axis=1, keepdims=True) - log_p
            draft_logprob[:, p : p + 1] = draft
            product = product * (1.0 / (1.0 + jnp.exp(limits[:, p : p + 1] - draft)))
            total = total + product
    expected[...] = column_to_row(total, seqs)[:, 0:seqs]
    z_loss[...] = jnp.sum(squares, axis=1, keepdims=True) * (Z_WEIGHT / (128 * POSITIONS))


def local(hidden, head_weight, drafts, cutoffs):
    f32, bf16 = jnp.float32, jnp.bfloat16
    dma = pltpu.SemaphoreType.DMA
    vmem = pl.BlockSpec(memory_space=pltpu.VMEM)
    hbm = pl.BlockSpec(memory_space=pl.ANY)
    packed = pl.pallas_call(
        verify_kernel,
        out_shape=jax.ShapeDtypeStruct((8, 128), f32),
        in_specs=[hbm, hbm, vmem],
        out_specs=vmem,
        scratch_shapes=[
            pltpu.VMEM((TILES, NX, ROWS, TILE), bf16),
            pltpu.VMEM((TILES * TILE, WIDTH), bf16),
            pltpu.VMEM((TILES * TILE, WIDTH), bf16),
            pltpu.VMEM((NX * ROWS, WIDTH), f32),
            pltpu.VMEM((NX * ROWS, WIDTH), f32),
            pltpu.VMEM((NX, ROWS, 128), f32),
            pltpu.VMEM((8, 128), f32),
            pltpu.VMEM((NZ - 1, 8, 128), f32),
            pltpu.VMEM((8, 128), f32),
            pltpu.VMEM((NX * NY - 1, 8, 128), f32),
            pltpu.VMEM((8, 128), f32),
            pltpu.VMEM((8, 128), f32),
            dma, dma, dma, dma,
            dma((9,)), dma((9,)), dma((6,)), dma((6,)),
            dma((2, REGION)), dma((REGION,)), dma((27,)),
            dma((2,)), dma((2,)), dma, dma,
        ],
        compiler_params=pltpu.CompilerParams(
            collective_id=0, has_side_effects=True, vmem_limit_bytes=60 * 2**20
        ),
        name="verify",
    )(hidden, head_weight, drafts)
    log_norm, draft_logprob, expected, z_loss = pl.pallas_call(
        finish_kernel,
        out_shape=[
            jax.ShapeDtypeStruct((16, POSITIONS), f32),
            jax.ShapeDtypeStruct((16, DRAFTS), f32),
            jax.ShapeDtypeStruct((1, 16), f32),
            jax.ShapeDtypeStruct((1, 1), f32),
        ],
        in_specs=[vmem, vmem],
        out_specs=[vmem] * 4,
        name="finish",
    )(packed, cutoffs)
    return log_norm, draft_logprob, expected.reshape(16), z_loss.reshape(())


def solution(mesh):
    split = Mesh(mesh.devices.reshape(NX, 2, NY, NZ), AXES)
    dp, everything = ("x", "core"), ("x", "core", "y", "z")
    return jax.shard_map(
        local,
        mesh=split,
        in_specs=(P(dp, None), P(None, everything), P(), P(dp, None)),
        out_specs=(P(dp, None), P(dp, None), P(dp), P()),
        check_vma=False,
    )
```

time: 126 us -> 54.2 us (0.43)
  the two profiles are of different devices: /device:TPU:2 before, /device:TPU:1 now
where the time goes in v1:
time: 54.2 us; the launch traced here: 53.9 us
  Pallas kernels  48.4 us (89%)
  local copies, waits for them, and re-layouts  4.79 us (9%)
  between operations  0.66 us (1%)
    pallas_call x1, Pallas kernels, local(): pl.pallas_call(verify_kernel, out_shape=jax.ShapeDtypeStruct((8, 128), f3...  46.9 us
    unnamed x6, local copies, waits for them, and re-layouts  4.79 us
    pallas_call x1, Pallas kernels, local(): pl.pallas_call(finish_kernel, out_shape=[jax.ShapeDtypeStruct((16, POSITI...  1.5 us

profile of v1, /device:TPU:1, one launch (start us, length us, event | category | flops | bytes accessed | tf_op | source)
XLA Modules:
  0.0 53.9 jit_solution(9792432975943444455)
XLA Ops:
  0.6 0.0 copy-start
  0.6 1.4 %copy.8.drafts = s32[128,4]{1,0:T(8,128)} copy(s32[128,4]{0,1:T(4,128)} %param.6) | data formatting | bytes 4096 | tf_op args[2]
  2.0 46.9 %verify.1.packed = f32[8,128]{1,0:T(8,128)} custom-call(bf16[80,4608]{1,0:T(8,128)(2,1)} %hidden.1, bf16[4608,512]{1,0:T(8,128)(2,1)} %weight.1, s32[128,4]{1,0:T(8,128)} %copy.8.drafts), custom_call_target="tpu_custom_call" | custom-call | tf_op jit(solution)/shard_map/verify/pallas_call | solution.py:268
  49.0 0.0 copy-done
  49.0 0.7 %copy.9.cutoffs = s32[16,4]{1,0:T(8,128)} copy(s32[16,4]{0,1:T(4,128)S(1)} %copy-done) | data formatting | bytes 512 | tf_op args[3]
  49.6 1.5 %finish.1 = (f32[16,5]{1,0:T(8,128)}, f32[16,4]{1,0:T(8,128)}, f32[1,16]{1,0:T(1,128)}, f32[1,1]{1,0:T(1,128)}) custom-call(f32[8,128]{1,0:T(8,128)} %verify.1.packed, s32[16,4]{1,0:T(8,128)} %copy.9.cutoffs), custom_call_target="tpu_custom_call" | custom-call | tf_op jit(solution)/shard_map/finish/pallas_call | solution.py:296
  51.1 1.4 %copy.10 = f32[16,5]{0,1:T(8,128)} copy(f32[16,5]{1,0:T(8,128)} %get-tuple-element.12) | data formatting | bytes 640
  52.5 1.3 %copy.11 = f32[16,4]{0,1:T(4,128)} copy(f32[16,4]{1,0:T(8,128)} %get-tuple-element.13) | data formatting | bytes 512
Async XLA Ops:
  0.6 48.3 %copy-start = (s32[16,4]{0,1:T(4,128)S(1)}, s32[16,4]{0,1:T(4,128)}, u32[]{:S(2)}) copy-start(s32[16,4]{0,1:T(4,128)} %param.7) | copy-start | bytes 772

commit v2 on v1

v2 whole, which is shorter than its diff:
```python
import functools

import jax
import jax.numpy as jnp
from jax import lax
from jax.experimental import pallas as pl
from jax.experimental.pallas import tpu as pltpu
from jax.sharding import Mesh
from jax.sharding import PartitionSpec as P

DRAFTS = 4
POSITIONS = 5
AXES = ("x", "core", "y", "z")
NX, NY, NZ = 4, 8, 8
MESH = pl.DeviceIdType.MESH

SOFT_CAP = 30.0
Z_WEIGHT = 0.001

ROWS = 80
WIDTH = 512
TILE = 256
TILES = 18
REGION = 3
DIRECT = 4 * REGION
BEHIND = (0, 1, 3, 2)


def column_to_row(column, rows):
    at = lax.broadcasted_iota(jnp.int32, (rows, 128), 0)
    lane = lax.broadcasted_iota(jnp.int32, (rows, 128), 1)
    return jnp.sum(jnp.where(at == lane, column, 0.0), axis=0, keepdims=True)


def verify_kernel(
    hidden, weight, drafts, out,
    held, own_w, partner_w, acc_own, acc_partner, wanted, ids, part, z_in, xy_out, xy_in, log_part, log_in,
    load_sem, small_sem, w_sem, w_send, w_recv, color_recv, color_send, direct_recv, direct_send,
    near_recv, far_recv, plane_send, red_send, red_recv, fin_send, fin_recv, round_a, round_b, round_c,
):
    x, core, y, z = (lax.axis_index(a) for a in AXES)
    step = 1 - 2 * core

    def ahead(n):
        return lax.rem(x + n * step + NX, NX)

    def at(dx=0, dy=0, dz=0):
        return (
            ahead(dx) if dx else x,
            core,
            lax.rem(y + dy + NY, NY) if dy else y,
            lax.rem(z + dz + NZ, NZ) if dz else z,
        )

    partner = (x, 1 - core, y, z)
    front, back = at(dx=1), at(dx=-1)
    colour = lax.rem(y + 2 * z, 4)
    mine = REGION * colour
    sent = []

    def remote(src, dst, send, recv, to):
        copy = pltpu.make_async_remote_copy(
            src_ref=src, dst_ref=dst, send_sem=send, recv_sem=recv, device_id=to, device_id_type=MESH
        )
        copy.start()
        return copy

    def signal(sem, peers):
        for peer in peers:
            pl.semaphore_signal(sem, inc=1, device_id=peer, device_id_type=MESH)
        return len(peers)

    neighbours = [front, back, at(dy=1), at(dy=-1), at(dz=1), at(dz=-1)]
    barrier = pltpu.get_barrier_semaphore()
    greeted = signal(barrier, neighbours + [partner])

    for t in range(TILES):
        pltpu.make_async_copy(hidden.at[:, pl.ds(t * TILE, TILE)], held.at[t, 0], load_sem).start()
    load_ids = pltpu.make_async_copy(drafts, wanted, small_sem)
    load_ids.start()
    load_w = pltpu.make_async_copy(weight, own_w, w_sem)
    load_w.start()
    pltpu.make_async_copy(held.at[:, 0], held.at[:, 0], load_sem).wait()
    pl.semaphore_wait(barrier, greeted)

    color_in = {}
    for i, (to, place, t) in enumerate(
        [(front, 1, 0), (back, 2, 2), (front, 1, 1), (back, 2, 0), (front, 1, 2), (back, 2, 1)]
    ):
        copy = remote(held.at[mine + t, 0], held.at[mine + t, place], color_send.at[i], color_recv.at[i], to)
        color_in[place, t] = copy
        sent.append(copy)

    direct_in = {}

    def direct(to, source, place, t):
        i = len(direct_in)
        copy = remote(
            held.at[DIRECT + t, source], held.at[DIRECT + t, place], direct_send.at[i], direct_recv.at[i], to
        )
        direct_in[place, t] = copy
        sent.append(copy)

    low, high = range(REGION), range(REGION, 2 * REGION)
    for i in range(REGION):
        direct(front, 0, 1, low[i])
        direct(back, 0, 2, high[i])
    w_copy = remote(weight, partner_w, w_send, w_recv, partner)
    sent.append(w_copy)

    signal(round_a, neighbours)

    load_ids.wait()
    row = lax.broadcasted_iota(jnp.int32, (ROWS, 128), 0)
    lane = lax.broadcasted_iota(jnp.int32, (ROWS, 128), 1)
    chosen = wanted[...].astype(jnp.float32)
    bonus = lax.rem(lax.broadcasted_iota(jnp.int32, (ROWS, 1), 0), POSITIONS) == DRAFTS
    for place in range(NX):
        block = 2 * ahead(-BEHIND[place]) + core
        spread = jnp.zeros((ROWS, 128), jnp.float32)
        for p in range(DRAFTS):
            here = row + ROWS * block == lane * POSITIONS + p
            spread += jnp.where(here, chosen[p : p + 1], 0.0)
        found = jnp.sum(spread, axis=1, keepdims=True)
        ids[place] = jnp.broadcast_to(jnp.where(bonus, -1.0, found), (ROWS, 128)).astype(jnp.int32)

    plane_count = [0]

    def forward(place, t):
        piece = held.at[mine + t, place]
        toward = at(dz=1) if t < 2 else at(dz=-1)
        recv = far_recv if place == 3 else near_recv
        for k, to in ((0, at(dy=1)), (1, at(dy=-1)), (2, toward)):
            sent.append(remote(piece, piece, plane_send.at[plane_count[0]], recv.at[k, t], to))
            plane_count[0] += 1

    relays = {(1, 0): front, (2, 2): back, (1, 1): front}
    for place, t in [(1, 0), (2, 2), (1, 1), (2, 0), (1, 2), (2, 1)]:
        color_in[place, t].wait_recv()
        if (place, t) in relays:
            i = 6 + t
            copy = remote(
                held.at[mine + t, place], held.at[mine + t, 3], color_send.at[i], color_recv.at[i], relays[place, t]
            )
            color_in[3, t] = copy
            sent.append(copy)
        forward(place, t)
    for i in range(REGION):
        direct(front, 0, 1, high[i])
        direct(back, 0, 2, low[i])
    pl.semaphore_wait(round_a, len(neighbours))
    count_b = signal(round_b, [at(dy=2), at(dy=-2), at(dz=2), at(dz=-2)])
    for i in range(REGION):
        direct_in[1, low[i]].wait_recv()
        direct(front, 1, 3, low[i])
        direct_in[2, high[i]].wait_recv()
        direct(back, 2, 3, high[i])
    for t in (0, 2, 1):
        color_in[3, t].wait_recv()
        forward(3, t)
    pl.semaphore_wait(round_b, count_b)
    count_c = signal(round_c, [at(dx=1), at(dx=-1), at(dx=2)])

    load_w.wait()
    w_copy.wait_recv()
    near, far = (0, 3), (3, 1)

    def multiply(span, tiles, start=False):
        first, count = span
        rows = pl.ds(first * ROWS, count * ROWS)
        for weights, total in ((own_w, acc_own), (partner_w, acc_partner)):
            value = None if start else total[rows, :]
            for t in tiles:
                depth = pl.ds(pl.multiple_of(t * TILE, TILE), TILE)
                product = jnp.dot(
                    held[t, pl.ds(first, count)].reshape(count * ROWS, TILE),
                    weights[depth, :],
                    preferred_element_type=jnp.float32,
                )
                value = product if value is None else value + product
            total[rows, :] = value

    def arrived(t, span, sem):
        piece = held.at[t, pl.ds(*span)]
        pltpu.make_async_copy(piece, piece, sem).wait()

    vocab = y * NZ + z
    columns = lax.broadcasted_iota(jnp.int32, (ROWS, 128), 1)

    def summed(place):
        exp_sum = jnp.zeros((ROWS, 128), jnp.float32)
        pick_sum = jnp.zeros((ROWS, 128), jnp.float32)
        for total, at_core in ((acc_own, core), (acc_partner, 1 - core)):
            offset = ((2 * x + at_core) * (NY * NZ) + vocab) * WIDTH
            for j in range(WIDTH // 128):
                logits = total[pl.ds(place * ROWS, ROWS), pl.ds(j * 128, 128)]
                capped = SOFT_CAP * jnp.tanh(logits * (1.0 / SOFT_CAP))
                exp_sum += jnp.exp(capped)
                pick_sum += jnp.where(columns + (offset + j * 128) == ids[place], capped, 0.0)
        k = BEHIND[place]
        part[pl.ds(k, 1), :] = column_to_row(jnp.sum(exp_sum, axis=1, keepdims=True), ROWS)
        part[pl.ds(NX + k, 1), :] = column_to_row(jnp.sum(pick_sum, axis=1, keepdims=True), ROWS)

    def region(shift):
        return REGION * lax.rem(colour + shift, 4)

    own_tiles = [mine + t for t in range(REGION)]
    multiply(near, own_tiles, start=True)
    multiply(far, own_tiles, start=True)
    sides = ((2, 2), (0, 3), (1, 1))
    for k, shift in sides:
        tiles = [region(shift) + t for t in range(REGION)]
        for t in range(REGION):
            arrived(tiles[t], (1, 2), near_recv.at[k, t])
        multiply(near, tiles)
    for group, place in ((low, 2), (high, 1)):
        for t in group:
            direct_in[place, t].wait_recv()
        multiply(near, [DIRECT + t for t in group])
    tiles = [region(2) + t for t in range(REGION)]
    for t in range(REGION):
        arrived(tiles[t], (3, 1), far_recv.at[2, t])
    multiply(far, tiles)
    pl.semaphore_wait(round_c, count_c)
    for place in (0, 1, 2):
        summed(place)
    for i, t in enumerate((0, 2, 1)):
        tiles = []
        for group in (low, high):
            direct_in[3, group[i]].wait_recv()
            tiles.append(DIRECT + group[i])
        for k, shift in sides[1:]:
            tiles.append(region(shift) + t)
            arrived(tiles[-1], (3, 1), far_recv.at[k, t])
        multiply(far, tiles)
    summed(3)

    for d in range(1, NZ):
        remote(part, z_in.at[d - 1], red_send.at[0], red_recv.at[0], at(dz=d))
    pltpu.make_async_copy(z_in, z_in, red_recv.at[0]).wait()
    plane = part[...] + jnp.sum(z_in[...], axis=0)
    for a in range(NX):
        k = NX + (-a) % NX
        xy_out[a, 0:NX] = plane[0:NX]
        xy_out[a, NX : NX + 1] = plane[k : k + 1]
    used = pl.ds(0, NX + 1)
    for a in range(NX):
        for b in range(NY):
            if a or b:
                remote(
                    xy_out.at[a, used], xy_in.at[a * NY + b - 1, used], red_send.at[1], red_recv.at[1], at(dx=a, dy=b)
                )
    pltpu.make_async_copy(xy_in.at[:, used], xy_in.at[:, used], red_recv.at[1]).wait()
    from_x = []
    for a in range(NX):
        first = max(a * NY - 1, 0)
        count = NY if a else NY - 1
        value = jnp.sum(xy_in[pl.ds(first, count), 0 : NX + 1], axis=0)
        from_x.append(value + xy_out[0, 0 : NX + 1] if a == 0 else value)
    totals = []
    for slot in range(NX):
        value = from_x[0][slot : slot + 1]
        for a in range(1, NX):
            k = (slot - a) % NX
            value += from_x[a][k : k + 1]
        totals.append(value)
    picked = functools.reduce(jnp.add, [value[NX : NX + 1] for value in from_x])
    valid = lax.broadcasted_iota(jnp.int32, (1, 128), 1) < ROWS
    logs = [jnp.log(jnp.where(valid, value, 1.0)) for value in totals]
    squares = functools.reduce(jnp.add, [value * value for value in logs])
    log_part[...] = jnp.broadcast_to(squares, (8, 128))
    fin = remote(log_part, log_in, fin_send, fin_recv, partner)
    out[pl.ds(0, 1), :] = logs[0]
    out[pl.ds(1, 1), :] = picked
    out[pl.ds(3, 5), :] = jnp.zeros((5, 128), jnp.float32)
    pltpu.make_async_copy(z_in, z_in, red_send.at[0]).wait()
    pltpu.make_async_copy(xy_in.at[:, used], xy_in.at[:, used], red_send.at[1]).wait()
    for copy in sent:
        copy.wait_send()
    fin.wait()
    out[pl.ds(2, 1), :] = squares + log_in[pl.ds(0, 1), :]


def finish_kernel(packed, cutoffs, log_norm, draft_logprob, expected, z_loss):
    seqs = 16
    at = lax.broadcasted_iota(jnp.int32, (seqs, 128), 0)
    lane = lax.broadcasted_iota(jnp.int32, (seqs, 128), 1)
    logs, picked, squares = packed[0:1], packed[1:2], packed[2:3]
    product = jnp.ones((1, seqs), jnp.float32)
    total = jnp.zeros((1, seqs), jnp.float32)
    for p in range(POSITIONS):
        here = lane == at * POSITIONS + p

        def of(values):
            return column_to_row(jnp.sum(jnp.where(here, values, 0.0), axis=1, keepdims=True), seqs)[:, 0:seqs]

        log_p = of(logs)
        log_norm[p : p + 1, :] = log_p
        if p < DRAFTS:
            draft = of(picked) - log_p
            draft_logprob[p : p + 1, :] = draft
            limit = cutoffs[p : p + 1, :].astype(jnp.float32) * (1.0 / 1024.0)
            product = product * (1.0 / (1.0 + jnp.exp(limit - draft)))
            total = total + product
    expected[...] = total
    z_loss[...] = jnp.sum(squares, axis=1, keepdims=True) * (Z_WEIGHT / (128 * POSITIONS))


def local(hidden, head_weight, drafts, cutoffs):
    f32, bf16 = jnp.float32, jnp.bfloat16
    dma, regular = pltpu.SemaphoreType.DMA, pltpu.SemaphoreType.REGULAR
    vmem = pl.BlockSpec(memory_space=pltpu.VMEM)
    hbm = pl.BlockSpec(memory_space=pl.ANY)
    packed = pl.pallas_call(
        verify_kernel,
        out_shape=jax.ShapeDtypeStruct((8, 128), f32),
        in_specs=[hbm, hbm, hbm],
        out_specs=vmem,
        scratch_shapes=[
            pltpu.VMEM((TILES, NX, ROWS, TILE), bf16),
            pltpu.VMEM((TILES * TILE, WIDTH), bf16),
            pltpu.VMEM((TILES * TILE, WIDTH), bf16),
            pltpu.VMEM((NX * ROWS, WIDTH), f32),
            pltpu.VMEM((NX * ROWS, WIDTH), f32),
            pltpu.VMEM((DRAFTS, 128), jnp.int32),
            pltpu.VMEM((NX, ROWS, 128), jnp.int32),
            pltpu.VMEM((8, 128), f32),
            pltpu.VMEM((NZ - 1, 8, 128), f32),
            pltpu.VMEM((NX, 8, 128), f32),
            pltpu.VMEM((NX * NY - 1, 8, 128), f32),
            pltpu.VMEM((8, 128), f32),
            pltpu.VMEM((8, 128), f32),
            dma, dma, dma, dma, dma,
            dma((9,)), dma((9,)), dma((18,)), dma((18,)),
            dma((3, REGION)), dma((3, REGION)), dma((27,)),
            dma((2,)), dma((2,)), dma, dma,
            regular, regular, regular,
        ],
        compiler_params=pltpu.CompilerParams(
            collective_id=0, has_side_effects=True, vmem_limit_bytes=60 * 2**20
        ),
        name="verify",
    )(hidden, head_weight, drafts.T)
    log_norm, draft_logprob, expected, z_loss = pl.pallas_call(
        finish_kernel,
        out_shape=[
            jax.ShapeDtypeStruct((POSITIONS, 16), f32),
            jax.ShapeDtypeStruct((DRAFTS, 16), f32),
            jax.ShapeDtypeStruct((1, 16), f32),
            jax.ShapeDtypeStruct((1, 1), f32),
        ],
        in_specs=[vmem, vmem],
        out_specs=[vmem] * 4,
        name="finish",
    )(packed, cutoffs.T)
    return log_norm.T, draft_logprob.T, expected.reshape(16), z_loss.reshape(())


def solution(mesh):
    split = Mesh(mesh.devices.reshape(NX, 2, NY, NZ), AXES)
    dp, everything = ("x", "core"), ("x", "core", "y", "z")
    return jax.shard_map(
        local,
        mesh=split,
        in_specs=(P(dp, None), P(None, everything), P(), P(dp, None)),
        out_specs=(P(dp, None), P(dp, None), P(dp), P()),
        check_vma=False,
    )
```

time: 54.2 us -> 44.1 us (0.81)
  Pallas kernels: 48.4 us -> 43.4 us
  local copies, waits for them, and re-layouts: 4.79 us -> 0 us
    pallas_call x1, Pallas kernels: 46.9 us -> 42 us  [local(): pl.pallas_call(verify_kernel, out_shape=jax.ShapeDtypeStruct((8, 128), f3...]
    unnamed x6 -> x0, local copies, waits for them, and re-layouts: 4.79 us -> none
where the time goes in v2:
time: 44.1 us; the launch traced here: 44 us
  Pallas kernels  43.4 us (98%)
  between operations  0.64 us (1%)
    pallas_call x1, Pallas kernels, local(): pl.pallas_call(verify_kernel, out_shape=jax.ShapeDtypeStruct((8, 128), f3...  42 us
    pallas_call x1, Pallas kernels, local(): pl.pallas_call(finish_kernel, out_shape=[jax.ShapeDtypeStruct((POSITIONS,...  1.39 us

profile of v2, /device:TPU:1, one launch (start us, length us, event | category | flops | bytes accessed | tf_op | source)
XLA Modules:
  0.0 44.0 jit_solution(8324930949023304760)
XLA Ops:
  0.6 42.0 %verify.1.packed = f32[8,128]{1,0:T(8,128)} custom-call(bf16[80,4608]{1,0:T(8,128)(2,1)} %hidden.1, bf16[4608,512]{1,0:T(8,128)(2,1)} %weight.1, s32[4,128]{1,0:T(4,128)} %bitcast.6), custom_call_target="tpu_custom_call" | custom-call | tf_op jit(solution)/shard_map/verify/pallas_call | solution.py:314
  42.6 1.4 %finish.1 = (f32[5,16]{1,0:T(8,128)}, f32[4,16]{1,0:T(4,128)}, f32[1,16]{1,0:T(1,128)}, f32[1,1]{1,0:T(1,128)}) custom-call(f32[8,128]{1,0:T(8,128)} %verify.1.packed, s32[4,16]{1,0:T(4,128)} %bitcast.7), custom_call_target="tpu_custom_call" | custom-call | tf_op jit(solution)/shard_map/finish/pallas_call | solution.py:344

commit v3 on v2

--- a/solution.py
+++ b/solution.py
@@ -23,6 +23,7 @@
 TILES = 18
 REGION = 3
 DIRECT = 4 * REGION
+PAIR = 2
 BEHIND = (0, 1, 3, 2)
 
 
@@ -36,7 +37,7 @@
     hidden, weight, drafts, out,
     held, own_w, partner_w, acc_own, acc_partner, wanted, ids, part, z_in, xy_out, xy_in, log_part, log_in,
     load_sem, small_sem, w_sem, w_send, w_recv, color_recv, color_send, direct_recv, direct_send,
-    near_recv, far_recv, plane_send, red_send, red_recv, fin_send, fin_recv, round_a, round_b, round_c,
+    near_recv, far_recv, plane_send, shared_recv, shared_send, red_send, red_recv, fin_send, fin_recv, round_a, round_b, round_c,
 ):
     x, core, y, z = (lax.axis_index(a) for a in AXES)
     step = 1 - 2 * core
@@ -93,16 +94,20 @@
 
     direct_in = {}
 
-    def direct(to, source, place, t):
+    def direct(to, source, place, t, key=None):
         i = len(direct_in)
         copy = remote(
             held.at[DIRECT + t, source], held.at[DIRECT + t, place], direct_send.at[i], direct_recv.at[i], to
         )
-        direct_in[place, t] = copy
+        direct_in[place, t if key is None else key] = copy
         sent.append(copy)
 
-    low, high = range(REGION), range(REGION, 2 * REGION)
-    for i in range(REGION):
+    parity = lax.rem(z, 2)
+    over_x, over_z = 2 * PAIR + parity, 2 * PAIR + 1 - parity
+    direct(front, 0, 1, over_x, "x")
+    direct(back, 0, 2, over_x, "x")
+    low, high = range(PAIR), range(PAIR, 2 * PAIR)
+    for i in range(PAIR):
         direct(front, 0, 1, low[i])
         direct(back, 0, 2, high[i])
     w_copy = remote(weight, partner_w, w_send, w_recv, partner)
@@ -145,12 +150,23 @@
             color_in[3, t] = copy
             sent.append(copy)
         forward(place, t)
-    for i in range(REGION):
+
+    def share(place):
+        piece = held.at[DIRECT + over_x, place]
+        to = at(dz=-1) if place == 2 else at(dz=1)
+        sent.append(remote(piece, piece, shared_send.at[place - 1], shared_recv.at[place - 1], to))
+
+    direct_in[1, "x"].wait_recv()
+    share(1)
+    direct_in[2, "x"].wait_recv()
+    direct(back, 2, 3, over_x, "x")
+    share(2)
+    for i in range(PAIR):
         direct(front, 0, 1, high[i])
         direct(back, 0, 2, low[i])
     pl.semaphore_wait(round_a, len(neighbours))
     count_b = signal(round_b, [at(dy=2), at(dy=-2), at(dz=2), at(dz=-2)])
-    for i in range(REGION):
+    for i in range(PAIR):
         direct_in[1, low[i]].wait_recv()
         direct(front, 1, 3, low[i])
         direct_in[2, high[i]].wait_recv()
@@ -158,6 +174,8 @@
     for t in (0, 2, 1):
         color_in[3, t].wait_recv()
         forward(3, t)
+    direct_in[3, "x"].wait_recv()
+    share(3)
     pl.semaphore_wait(round_b, count_b)
     count_c = signal(round_c, [at(dx=1), at(dx=-1), at(dx=2)])
 
@@ -213,10 +231,12 @@
         for t in range(REGION):
             arrived(tiles[t], (1, 2), near_recv.at[k, t])
         multiply(near, tiles)
+    for place in (1, 2):
+        arrived(DIRECT + over_z, (place, 1), shared_recv.at[place - 1])
     for group, place in ((low, 2), (high, 1)):
         for t in group:
             direct_in[place, t].wait_recv()
-        multiply(near, [DIRECT + t for t in group])
+    multiply(near, [DIRECT + t for t in range(2 * PAIR + 2)])
     tiles = [region(2) + t for t in range(REGION)]
     for t in range(REGION):
         arrived(tiles[t], (3, 1), far_recv.at[2, t])
@@ -226,16 +246,19 @@
         summed(place)
     for i, t in enumerate((0, 2, 1)):
         tiles = []
-        for group in (low, high):
+        for group in (low, high) if i < PAIR else ():
             direct_in[3, group[i]].wait_recv()
             tiles.append(DIRECT + group[i])
+        if i == PAIR:
+            arrived(DIRECT + over_z, (3, 1), shared_recv.at[2])
+            tiles += [DIRECT + 2 * PAIR, DIRECT + 2 * PAIR + 1]
         for k, shift in sides[1:]:
             tiles.append(region(shift) + t)
             arrived(tiles[-1], (3, 1), far_recv.at[k, t])
         multiply(far, tiles)
     summed(3)
 
-    for d in range(1, NZ):
+    for d in sorted(range(1, NZ), key=lambda d: -min(d, NZ - d)):
         remote(part, z_in.at[d - 1], red_send.at[0], red_recv.at[0], at(dz=d))
     pltpu.make_async_copy(z_in, z_in, red_recv.at[0]).wait()
     plane = part[...] + jnp.sum(z_in[...], axis=0)
@@ -244,12 +267,9 @@
         xy_out[a, 0:NX] = plane[0:NX]
         xy_out[a, NX : NX + 1] = plane[k : k + 1]
     used = pl.ds(0, NX + 1)
-    for a in range(NX):
-        for b in range(NY):
-            if a or b:
-                remote(
-                    xy_out.at[a, used], xy_in.at[a * NY + b - 1, used], red_send.at[1], red_recv.at[1], at(dx=a, dy=b)
-                )
+    pairs = [(a, b) for a in range(NX) for b in range(NY) if a or b]
+    for a, b in sorted(pairs, key=lambda p: -min(p[0], NX - p[0]) - min(p[1], NY - p[1])):
+        remote(xy_out.at[a, used], xy_in.at[a * NY + b - 1, used], red_send.at[1], red_recv.at[1], at(dx=a, dy=b))
     pltpu.make_async_copy(xy_in.at[:, used], xy_in.at[:, used], red_recv.at[1]).wait()
     from_x = []
     for a in range(NX):
@@ -310,7 +330,7 @@
     f32, bf16 = jnp.float32, jnp.bfloat16
     dma, regular = pltpu.SemaphoreType.DMA, pltpu.SemaphoreType.REGULAR
     vmem = pl.BlockSpec(memory_space=pltpu.VMEM)
-    hbm = pl.BlockSpec(memory_space=pl.ANY)
+    hbm = pl.BlockSpec(memory_space=pltpu.HBM)
     packed = pl.pallas_call(
         verify_kernel,
         out_shape=jax.ShapeDtypeStruct((8, 128), f32),
@@ -331,16 +351,16 @@
             pltpu.VMEM((8, 128), f32),
             pltpu.VMEM((8, 128), f32),
             dma, dma, dma, dma, dma,
-            dma((9,)), dma((9,)), dma((18,)), dma((18,)),
-            dma((3, REGION)), dma((3, REGION)), dma((27,)),
+            dma((9,)), dma((9,)), dma((15,)), dma((15,)),
+            dma((3, REGION)), dma((3, REGION)), dma((27,)), dma((3,)), dma((3,)),
             dma((2,)), dma((2,)), dma, dma,
             regular, regular, regular,
         ],
         compiler_params=pltpu.CompilerParams(
-            collective_id=0, has_side_effects=True, vmem_limit_bytes=60 * 2**20
+            collective_id=0, has_side_effects=True, vmem_limit_bytes=20 * 2**20
         ),
         name="verify",
-    )(hidden, head_weight, drafts.T)
+    )(*[pltpu.with_memory_space_constraint(v, pltpu.HBM) for v in (hidden, head_weight, drafts.T)])
     log_norm, draft_logprob, expected, z_loss = pl.pallas_call(
         finish_kernel,
         out_shape=[
@@ -351,6 +371,7 @@
         ],
         in_specs=[vmem, vmem],
         out_specs=[vmem] * 4,
+        compiler_params=pltpu.CompilerParams(vmem_limit_bytes=2**20),
         name="finish",
     )(packed, cutoffs.T)
     return log_norm.T, draft_logprob.T, expected.reshape(16), z_loss.reshape(())

time: 44.1 us -> 43.2 us (0.980)
  Pallas kernels: 43.4 us -> 42.4 us
    pallas_call x1, Pallas kernels: 1.39 us -> 0.7 us  [local(): pl.pallas_call(finish_kernel, out_shape=[jax.ShapeDtypeStruct((POSITIONS,...]
where the time goes in v3:
time: 43.2 us; the launch traced here: 43.1 us
  Pallas kernels  42.4 us (98%)
  between operations  0.66 us (2%)
    pallas_call x1, Pallas kernels, local(): pl.pallas_call(verify_kernel, out_shape=jax.ShapeDtypeStruct((8, 128), f3...  41.7 us

profile of v3, /device:TPU:1, one launch (start us, length us, event | category | flops | bytes accessed | tf_op | source)
XLA Modules:
  0.0 43.1 jit_solution(4066964600235599887)
XLA Ops:
  0.6 0.0 copy-start
  0.6 41.7 %verify.1.packed = f32[8,128]{1,0:T(8,128)S(1)} custom-call(bf16[80,4608]{1,0:T(8,128)(2,1)} %hidden.1, bf16[4608,512]{1,0:T(8,128)(2,1)} %weight.1, s32[4,128]{1,0:T(4,128)} %bitcast.7), custom_call_target="tpu_custom_call" | custom-call | tf_op jit(solution)/shard_map/verify/pallas_call | solution.py:334
  42.4 0.0 copy-done
  42.4 0.7 %finish.1 = (f32[5,16]{1,0:T(8,128)}, f32[4,16]{1,0:T(4,128)}, f32[1,16]{1,0:T(1,128)}, f32[1,1]{1,0:T(1,128)}) custom-call(f32[8,128]{1,0:T(8,128)S(1)} %verify.1.packed, s32[4,16]{1,0:T(4,128)S(1)} %bitcast.6), custom_call_target="tpu_custom_call" | custom-call | tf_op jit(solution)/shard_map/finish/pallas_call | solution.py:364
Async XLA Ops:
  0.6 41.7 %copy-start = (s32[16,4]{0,1:T(4,128)S(1)}, s32[16,4]{0,1:T(4,128)}, u32[]{:S(2)}) copy-start(s32[16,4]{0,1:T(4,128)} %param.7) | copy-start | bytes 772

commit v4 on v3

--- a/solution.py
+++ b/solution.py
@@ -35,15 +35,13 @@
 
 def verify_kernel(
     hidden, weight, drafts, out,
-    held, own_w, partner_w, acc_own, acc_partner, wanted, ids, part, z_in, xy_out, xy_in, log_part, log_in,
+    held, own_w, partner_w, acc_own, acc_partner, wanted, ids, part, both, z_in, xy_out, xy_in, result,
     load_sem, small_sem, w_sem, w_send, w_recv, color_recv, color_send, direct_recv, direct_send,
-    near_recv, far_recv, plane_send, shared_recv, shared_send, red_send, red_recv, fin_send, fin_recv, round_a, round_b, round_c,
+    near_recv, far_recv, plane_send, shared_recv, shared_send, red_send, red_recv, hand_send, hand_recv, fin_send, fin_recv, round_a, round_b, round_c,
 ):
     x, core, y, z = (lax.axis_index(a) for a in AXES)
-    step = 1 - 2 * core
-
     def ahead(n):
-        return lax.rem(x + n * step + NX, NX)
+        return lax.rem(x + n + NX, NX)
 
     def at(dx=0, dy=0, dz=0):
         return (
@@ -258,47 +256,71 @@
         multiply(far, tiles)
     summed(3)
 
-    for d in sorted(range(1, NZ), key=lambda d: -min(d, NZ - d)):
-        remote(part, z_in.at[d - 1], red_send.at[0], red_recv.at[0], at(dz=d))
-    pltpu.make_async_copy(z_in, z_in, red_recv.at[0]).wait()
-    plane = part[...] + jnp.sum(z_in[...], axis=0)
-    for a in range(NX):
-        k = NX + (-a) % NX
-        xy_out[a, 0:NX] = plane[0:NX]
-        xy_out[a, NX : NX + 1] = plane[k : k + 1]
+    hand_over = pltpu.make_async_remote_copy(
+        src_ref=part, dst_ref=both.at[1], send_sem=hand_send, recv_sem=hand_recv, device_id=partner, device_id_type=MESH
+    )
+    hand_back = pltpu.make_async_remote_copy(
+        src_ref=result, dst_ref=out, send_sem=fin_send, recv_sem=fin_recv, device_id=partner, device_id_type=MESH
+    )
     used = pl.ds(0, NX + 1)
-    pairs = [(a, b) for a in range(NX) for b in range(NY) if a or b]
-    for a, b in sorted(pairs, key=lambda p: -min(p[0], NX - p[0]) - min(p[1], NY - p[1])):
-        remote(xy_out.at[a, used], xy_in.at[a * NY + b - 1, used], red_send.at[1], red_recv.at[1], at(dx=a, dy=b))
-    pltpu.make_async_copy(xy_in.at[:, used], xy_in.at[:, used], red_recv.at[1]).wait()
-    from_x = []
-    for a in range(NX):
-        first = max(a * NY - 1, 0)
-        count = NY if a else NY - 1
-        value = jnp.sum(xy_in[pl.ds(first, count), 0 : NX + 1], axis=0)
-        from_x.append(value + xy_out[0, 0 : NX + 1] if a == 0 else value)
-    totals = []
-    for slot in range(NX):
-        value = from_x[0][slot : slot + 1]
-        for a in range(1, NX):
-            k = (slot - a) % NX
-            value += from_x[a][k : k + 1]
-        totals.append(value)
-    picked = functools.reduce(jnp.add, [value[NX : NX + 1] for value in from_x])
-    valid = lax.broadcasted_iota(jnp.int32, (1, 128), 1) < ROWS
-    logs = [jnp.log(jnp.where(valid, value, 1.0)) for value in totals]
-    squares = functools.reduce(jnp.add, [value * value for value in logs])
-    log_part[...] = jnp.broadcast_to(squares, (8, 128))
-    fin = remote(log_part, log_in, fin_send, fin_recv, partner)
-    out[pl.ds(0, 1), :] = logs[0]
-    out[pl.ds(1, 1), :] = picked
-    out[pl.ds(3, 5), :] = jnp.zeros((5, 128), jnp.float32)
-    pltpu.make_async_copy(z_in, z_in, red_send.at[0]).wait()
-    pltpu.make_async_copy(xy_in.at[:, used], xy_in.at[:, used], red_send.at[1]).wait()
+
+    @pl.when(core == 0)
+    def _():
+        hand_over.start()
+
+    @pl.when(core == 1)
+    def _():
+        both[0] = part[...]
+        hand_over.wait_recv()
+        for d in sorted(range(1, NZ), key=lambda d: -min(d, NZ - d)):
+            remote(both, z_in.at[d - 1], red_send.at[0], red_recv.at[0], at(dz=d))
+        pltpu.make_async_copy(z_in, z_in, red_recv.at[0]).wait()
+        plane = both[...] + jnp.sum(z_in[...], axis=0)
+        for a in range(NX):
+            k = NX + (-a) % NX
+            for h in range(2):
+                xy_out[a, h, 0:NX] = plane[h, 0:NX]
+                xy_out[a, h, NX : NX + 1] = plane[h, k : k + 1]
+        pairs = [(a, b) for a in range(NX) for b in range(NY) if a or b]
+        for a, b in sorted(pairs, key=lambda p: -min(p[0], NX - p[0]) - min(p[1], NY - p[1])):
+            piece, into = xy_out.at[a, :, used], xy_in.at[a * NY + b - 1, :, used]
+            remote(piece, into, red_send.at[1], red_recv.at[1], at(dx=a, dy=b))
+        pltpu.make_async_copy(xy_in.at[:, :, used], xy_in.at[:, :, used], red_recv.at[1]).wait()
+        valid = lax.broadcasted_iota(jnp.int32, (1, 128), 1) < ROWS
+        kept, squares = [], jnp.zeros((1, 128), jnp.float32)
+        for h in range(2):
+            from_x = []
+            for a in range(NX):
+                first = max(a * NY - 1, 0)
+                count = NY if a else NY - 1
+                value = jnp.sum(xy_in[pl.ds(first, count), h, 0 : NX + 1], axis=0)
+                from_x.append(value + xy_out[0, h, 0 : NX + 1] if a == 0 else value)
+            for slot in range(NX):
+                value = functools.reduce(
+                    jnp.add, [from_x[a][(slot - a) % NX : (slot - a) % NX + 1] for a in range(NX)]
+                )
+                log = jnp.log(jnp.where(valid, value, 1.0))
+                squares += log * log
+                if slot == 0:
+                    kept.append((log, functools.reduce(jnp.add, [v[NX : NX + 1] for v in from_x])))
+        for into, (log, picked) in ((result, kept[1]), (out, kept[0])):
+            into[pl.ds(0, 1), :] = log
+            into[pl.ds(1, 1), :] = picked
+            into[pl.ds(2, 1), :] = squares
+            into[pl.ds(3, 5), :] = jnp.zeros((5, 128), jnp.float32)
+            if into is result:
+                hand_back.start()
+        pltpu.make_async_copy(z_in, z_in, red_send.at[0]).wait()
+        pltpu.make_async_copy(xy_in.at[:, :, used], xy_in.at[:, :, used], red_send.at[1]).wait()
+        hand_back.wait_send()
+
     for copy in sent:
         copy.wait_send()
-    fin.wait()
-    out[pl.ds(2, 1), :] = squares + log_in[pl.ds(0, 1), :]
+
+    @pl.when(core == 0)
+    def _():
+        hand_over.wait_send()
+        hand_back.wait_recv()
 
 
 def finish_kernel(packed, cutoffs, log_norm, draft_logprob, expected, z_loss):
@@ -345,15 +367,15 @@
             pltpu.VMEM((DRAFTS, 128), jnp.int32),
             pltpu.VMEM((NX, ROWS, 128), jnp.int32),
             pltpu.VMEM((8, 128), f32),
-            pltpu.VMEM((NZ - 1, 8, 128), f32),
-            pltpu.VMEM((NX, 8, 128), f32),
-            pltpu.VMEM((NX * NY - 1, 8, 128), f32),
-            pltpu.VMEM((8, 128), f32),
+            pltpu.VMEM((2, 8, 128), f32),
+            pltpu.VMEM((NZ - 1, 2, 8, 128), f32),
+            pltpu.VMEM((NX, 2, 8, 128), f32),
+            pltpu.VMEM((NX * NY - 1, 2, 8, 128), f32),
             pltpu.VMEM((8, 128), f32),
             dma, dma, dma, dma, dma,
             dma((9,)), dma((9,)), dma((15,)), dma((15,)),
             dma((3, REGION)), dma((3, REGION)), dma((27,)), dma((3,)), dma((3,)),
-            dma((2,)), dma((2,)), dma, dma,
+            dma((2,)), dma((2,)), dma, dma, dma, dma,
             regular, regular, regular,
         ],
         compiler_params=pltpu.CompilerParams(

time: 43.2 us -> 42.8 us (level)
    pallas_call x1, Pallas kernels: 41.7 us -> 41.3 us  [local(): pl.pallas_call(verify_kernel, out_shape=jax.ShapeDtypeStruct((8, 128), f3...]
where the time goes in v4:
time: 42.8 us; the launch traced here: 42.6 us
  Pallas kernels  42 us (98%)
  between operations  0.66 us (2%)
    pallas_call x1, Pallas kernels, local(): pl.pallas_call(verify_kernel, out_shape=jax.ShapeDtypeStruct((8, 128), f3...  41.3 us

profile of v4, /device:TPU:1, one launch (start us, length us, event | category | flops | bytes accessed | tf_op | source)
XLA Modules:
  0.0 42.6 jit_solution(330289989784790186)
XLA Ops:
  0.6 0.0 copy-start
  0.6 41.3 %verify.1.packed = f32[8,128]{1,0:T(8,128)S(1)} custom-call(bf16[80,4608]{1,0:T(8,128)(2,1)} %hidden.1, bf16[4608,512]{1,0:T(8,128)(2,1)} %weight.1, s32[4,128]{1,0:T(4,128)} %bitcast.7), custom_call_target="tpu_custom_call" | custom-call | tf_op jit(solution)/shard_map/verify/pallas_call | solution.py:356
  41.9 0.0 copy-done
  41.9 0.7 %finish.1 = (f32[5,16]{1,0:T(8,128)}, f32[4,16]{1,0:T(4,128)}, f32[1,16]{1,0:T(1,128)}, f32[1,1]{1,0:T(1,128)}) custom-call(f32[8,128]{1,0:T(8,128)S(1)} %verify.1.packed, s32[4,16]{1,0:T(4,128)S(1)} %bitcast.6), custom_call_target="tpu_custom_call" | custom-call | tf_op jit(solution)/shard_map/finish/pallas_call | solution.py:386
Async XLA Ops:
  0.6 41.3 %copy-start = (s32[16,4]{0,1:T(4,128)S(1)}, s32[16,4]{0,1:T(4,128)}, u32[]{:S(2)}) copy-start(s32[16,4]{0,1:T(4,128)} %param.7) | copy-start | bytes 772
